TPU v7x, 128 devices: a whole 4x4x4 slice. The times are simulated.
128 devices in a mesh: rep: 4 (over x), ep: 32 (over y, z, core).
Axes of the slice: x: 4, y: 4, z: 4, core: 2. Of those that a mesh axis runs over, the one named last changes fastest.
Arguments:
- q_latent: bfloat16 [1024, 128, 512], P(('rep', 'ep')), may hold values from -6 to 6
- q_rope: bfloat16 [1024, 128, 64], P(('rep', 'ep')), may hold values from -104 to 104
- cache_latent: bfloat16 [1024, 128, 512], P(('rep', 'ep')), may hold values from -6 to 6
- cache_rope: bfloat16 [1024, 128, 64], P(('rep', 'ep')), may hold values from -6 to 6
- cache_len: int32 [1024], P(('rep', 'ep')), may hold values from 32 to 128, as said below
- stream: bfloat16 [1024, 7168], P(('rep', 'ep')), may hold values from -6 to 6
- norm_gain: float32 [7168], replicated, may hold values from 0.1 to 1.9
- expert_ids: int32 [1024, 8], P(('rep', 'ep')), may hold values from 0 to 63, all different within a row; in each aligned block of 8 rows (0 to 7, 8 to 15, ...) at most 2 rows name the same one
- route_weights: bfloat16 [1024, 8], P(('rep', 'ep')), may hold values from 0.099609375 to 1
- w_gate: bfloat16 [64, 7168, 1024], P('ep', None, 'rep'), may hold values from -0.0625 to 0.0625
- w_up: bfloat16 [64, 7168, 1024], P('ep', None, 'rep'), may hold values from -0.0625 to 0.0625
- w_down: bfloat16 [64, 1024, 7168], P('ep', 'rep'), may hold values from -0.1875 to 0.1875
Outputs:
- attn_latent: bfloat16 [1024, 128, 512], P(('rep', 'ep'))
- layer_out: bfloat16 [1024, 7168], P(('rep', 'ep'))
Inputs may be any that keep to these rules, and one draw needn't show every extreme that they name: `expert_ids`: each row names 8 different experts; within the rows of one device no expert is named by more than 2 rows, a bound that some block reaches. `cache_len`: some row has all 128 positions live.
All inputs are finite; a program needn't handle non-finite values.
Results may differ from a plain program's by a relative error of at most 0.01.
Values may be sent and summed in bfloat16 or wider, within the bound.
No kernel may reach another device: no remote copies, remote signals or barrier semaphores. Data moves between devices by JAX's collectives and lax.ppermute only.
A program may use at most 128 MiB of HBM per device.

v0:
```python
import jax
import jax.numpy as jnp
from jax import lax
from jax.sharding import Mesh
from jax.sharding import PartitionSpec as P

EP = ("ep_0", "ep_1", "ep_2")
REP_EP = ("rep", "ep_0", "ep_1", "ep_2")
score_scale = 192.0 ** (-0.5)
norm_eps = 1e-06


def cut_along(shard, dim, count):
    before, after = (shard.shape[:dim], shard.shape[dim + 1 :])
    return jnp.moveaxis(shard.reshape(*before, count, -1, *after), dim, 0)


def in_order(tiles, dim):
    tiles = jnp.moveaxis(tiles, 0, dim)
    dims = tiles.shape
    return tiles.reshape(*dims[:dim], dims[dim] * dims[dim + 1], *dims[dim + 2 :])


def moved_by_axis(tiles, axes, turns):
    inside = tiles.shape[1:]
    result = tiles.reshape(*(lax.axis_size(a) for a in axes), *inside)
    for k in turns:
        result = lax.all_to_all(result, axes[k], k, k, tiled=True)
    return result.reshape(-1, *inside)


def core_and_chips(shard, groups, turns, split_dim, concat_dim):
    count = lax.axis_size(groups[0]) * lax.axis_size(groups[1])
    tiles = cut_along(shard, split_dim, count)
    return in_order(moved_by_axis(tiles, groups, turns), concat_dim)


def slot_ranks(route_table, expert_total):
    onehot = (route_table[..., None] == jnp.arange(expert_total, dtype=jnp.int32)).astype(jnp.int32)
    earlier = jnp.cumsum(onehot, axis=1) - onehot
    return jnp.sum(earlier * onehot, axis=-1)


def fill_slots(features, slot_index, row_index, slot_total):
    sources = jnp.zeros((slot_total,), jnp.int32).at[slot_index].set(row_index)
    filled = jnp.zeros((slot_total,), features.dtype).at[slot_index].set(1)
    return features[sources] * filled[:, None]


def expert_block(tokens_in, gate_part, up_part, down_part):
    gate_act = jnp.dot(tokens_in, gate_part, preferred_element_type=jnp.float32)
    up_act = jnp.dot(tokens_in, up_part, preferred_element_type=jnp.float32)
    hidden = (jax.nn.silu(gate_act) * up_act).astype(jnp.bfloat16)
    return jnp.dot(hidden, down_part, preferred_element_type=jnp.float32).astype(jnp.bfloat16)


def per_device(
    q_latent,
    q_rope,
    cache_latent,
    cache_rope,
    cache_len,
    stream,
    norm_gain,
    expert_ids,
    route_weights,
    w_gate,
    w_up,
    w_down,
):
    ep_count = lax.axis_size(EP)
    row_count, feature_dim = stream.shape
    local_count = w_gate.shape[0]
    top_count = expert_ids.shape[1]
    expert_total = local_count * ep_count
    capacity = max(2, 2 * row_count * top_count // expert_total)
    stream_f = stream.astype(jnp.float32)
    normed = (
        stream_f
        * lax.rsqrt(jnp.mean(stream_f * stream_f, axis=-1, keepdims=True) + norm_eps)
        * norm_gain
    ).astype(jnp.bfloat16)
    flat_routes = expert_ids.reshape(-1)
    rank_in = slot_ranks(flat_routes.reshape(1, -1), expert_total)[0]
    expert_slot = flat_routes % local_count * ep_count + flat_routes // local_count
    slot_index = expert_slot * capacity + rank_in
    row_index = jnp.arange(row_count * top_count, dtype=jnp.int32) // top_count
    slot_total = expert_total * capacity
    outgoing = fill_slots(normed, slot_index, row_index, slot_total).reshape(
        local_count, ep_count, capacity, feature_dim
    )
    incoming = core_and_chips(outgoing, (("ep_0", "ep_1"), "ep_2"), (1, 0), 1, 1)
    incoming = incoming.reshape(local_count, ep_count * capacity, feature_dim)
    scores = (
        jnp.einsum("ihl,itl->iht", q_latent, cache_latent, preferred_element_type=jnp.float32)
        + jnp.einsum("ihr,itr->iht", q_rope, cache_rope, preferred_element_type=jnp.float32)
    ) * score_scale
    valid_mask = (
        jnp.arange(cache_latent.shape[1], dtype=jnp.int32)[None, None, :] < cache_len[:, None, None]
    )
    scores = jnp.where(valid_mask, scores, -1e30)
    top_score = jnp.max(scores, axis=-1, keepdims=True)
    exponent = jnp.where(valid_mask, jnp.exp(scores - top_score), 0.0)
    attn_weights = (exponent / jnp.sum(exponent, axis=-1, keepdims=True)).astype(jnp.bfloat16)
    attn_latent = jnp.einsum(
        "iht,itl->ihl", attn_weights, cache_latent, preferred_element_type=jnp.float32
    ).astype(jnp.bfloat16)
    everyone = lax.all_gather(incoming, "rep", axis=1, tiled=True)
    partials = jax.vmap(expert_block)(everyone, w_gate, w_up, w_down)
    partials = lax.optimization_barrier(partials)
    summed = lax.psum_scatter(
        partials.astype(jnp.float32).astype(jnp.bfloat16), "rep", scatter_dimension=1, tiled=True
    ).astype(jnp.float32)
    returned = lax.all_to_all(
        summed.reshape(local_count, ep_count, capacity, feature_dim).astype(jnp.bfloat16),
        EP,
        split_axis=1,
        concat_axis=1,
        tiled=True,
    ).astype(jnp.float32)
    picked = returned.reshape(slot_total, feature_dim)[slot_index].reshape(
        row_count, top_count, feature_dim
    )
    expert_sum = jnp.einsum(
        "rk,rkd->rd", route_weights.astype(jnp.float32), picked, precision=lax.Precision.HIGHEST
    )
    layer_out = (stream_f + expert_sum).astype(jnp.bfloat16)
    return (attn_latent, layer_out)


def solution(mesh):
    torus = Mesh(mesh.devices.reshape(mesh.shape["rep"], 4, 4, 2), ("rep", "ep_0", "ep_1", "ep_2"))
    return jax.shard_map(
        per_device,
        mesh=torus,
        in_specs=(
            P(REP_EP, None, None),
            P(REP_EP, None, None),
            P(REP_EP, None, None),
            P(REP_EP, None, None),
            P(REP_EP),
            P(REP_EP, None),
            P(),
            P(REP_EP, None),
            P(REP_EP, None),
            P(EP, None, "rep"),
            P(EP, None, "rep"),
            P(EP, "rep", None),
        ),
        out_specs=(P(REP_EP, None, None), P(REP_EP, None)),
        check_vma=False,
    )
```

profile of v0, /device:TPU:1, one launch (start us, length us, event | category | flops | bytes accessed | tf_op | source)
XLA Modules:
  0.0 291.7 jit_solution(6912116747219094064)
XLA Ops:
  7.2 0.0 copy-start
  7.2 0.0 all-gather.2.cloned.1.call-start
  7.2 0.8 eq.29
  8.1 0.8 reshape.284
  8.8 0.1 fusion.20
  8.9 0.1 reduce_window_sum.11
  9.0 0.2 select_reduce_fusion
  9.2 0.8 scatter_custom_fusion
  10.0 1.1 fusion.16
  11.1 1.0 fusion.18
  12.1 1.7 gather_fusion
  13.8 1.7 gather.9
  15.5 1.0 scatter_custom_fusion.1
  16.5 0.1 mul.87
  16.7 3.1 %copy_multiply_fusion = bf16[2,32,1,2,7168]{4,3,0,1,2:T(2,128)(2,1)S(1)} fusion(bf16[2,32,1,2,7168]{4,3,1,0,2:T(2,128)(2,1)} %gather.9, bf16[2,32,2]{2,0,1:T(2,128)(2,1)S(1)} %copy.21), kind=kLoop, calls=%fused_computation.6 | loop fusion | flops 917504 | bytes 3670272 | tf_op jit(solution)/shard_map/mul | solution.py:47
  19.8 1.3 copy.23
  21.1 6.2 %all_to_all.15 = bf16[16,2,2,1,2,7168]{5,4,0,2,3,1:T(2,128)(2,1)S(1)} all-to-all(bf16[16,2,2,1,2,7168]{5,4,0,2,3,1:T(2,128)(2,1)S(1)} %copy.23), channel_id=1, replica_groups=mesh['rep'=4,'ep_0'=4,'ep_1'=4,'ep_2'=2] {'ep_2'}, dimensions={1} | all-to-all | bytes 3670016 | tf_op jit(solution)/shard_map/all_to_all | solution.py:28
  27.3 1.7 copy.24
  29.0 32.2 %all_to_all.16 = bf16[16,2,2,1,2,7168]{5,4,1,2,3,0:T(2,128)(2,1)S(1)} all-to-all(bf16[16,2,2,1,2,7168]{5,4,1,2,3,0:T(2,128)(2,1)S(1)} %copy.24), channel_id=1, replica_groups=mesh['rep'=4,'ep_0'=4,'ep_1'=4,'ep_2'=2] {'ep_0','ep_1'}, dimensions={0} | all-to-all | bytes 3670016 | tf_op jit(solution)/shard_map/all_to_all | solution.py:28
  61.2 1.3 copy.25
  62.5 1.3 copy.26
  63.8 1.7 reshape_reshape.4
  65.5 0.0 all-gather.2.cloned.1.call-update
  65.6 0.2 reduce-scatter.2.cloned.1.call-start
  65.8 73.1 %all-gather.2.cloned.1.call-done = bf16[2,256,7168]{2,1,0:T(8,128)(2,1)} async-done(((bf16[2,64,7168]{2,1,0:T(8,128)(2,1)}), bf16[2,256,7168]{2,1,0:T(8,128)(2,1)}) %all-gather.2.cloned.1.call-update) | async-done | bytes 7340048 | tf_op jit(solution)/shard_map/all_gather | solution.py:108
  138.9 7.2 %fusion.34 = f32[2,256,256]{2,1,0:T(8,128)S(1)} fusion(bf16[2,256,7168]{2,1,0:T(8,128)(2,1)} %all-gather.2.cloned.1.call-done, bf16[2,7168,256]{2,1,0:T(8,128)(2,1)} %param.21), kind=kOutput, calls=%fused_computation.65 | convolution fusion | flops 1879048192 | bytes 15204352 | tf_op jit(solution)/shard_map/vmap()/dot_general | solution.py:51
  146.1 14.3 %convolution_convert_fusion = bf16[2,256,7168]{2,1,0:T(8,128)(2,1)} fusion(bf16[2,256,7168]{2,1,0:T(8,128)(2,1)} %param.23, bf16[2,256,7168]{2,1,0:T(8,128)(2,1)} %all-gather.2.cloned.1.call-done, bf16[2,7168,256]{2,1,0:T(8,128)(2,1)} %param.22, f32[2,256,256]{2,1,0:T(8,128)S(1)} %fusion.34), kind=kOutput, calls=%fused_computation.5 | convolution fusion | flops 3762552832 | bytes 29884416 | tf_op jit(solution)/shard_map/vmap()/dot_general | solution.py:54
  160.5 0.0 reduce-scatter.2.cloned.1.call-update
  160.5 73.6 %reduce-scatter.2.cloned.1.call-done = bf16[2,64,7168]{2,1,0:T(8,128)(2,1)} async-done(((bf16[2,256,7168]{2,1,0:T(8,128)(2,1)}), bf16[2,64,7168]{2,1,0:T(8,128)(2,1)}) %reduce-scatter.2.cloned.1.call-update) | async-done | bytes 1835024 | tf_op jit(solution)/shard_map/reduce_scatter | solution.py:111
  234.1 3.9 %convert_element_type.52 = bf16[2,32,2,7168]{3,2,1,0:T(2,128)(2,1)S(1)} reshape(bf16[2,64,7168]{2,1,0:T(8,128)(2,1)} %reduce-scatter.2.cloned.1.call-done) | data formatting | bytes 3670016 | tf_op jit(solution)/shard_map/convert_element_type | solution.py:115
  238.0 2.5 copy.27
  240.5 0.0 copy-start.5
  240.5 7.9 %all-to-all-start.2 = ((bf16[2,32,2,7168]{3,2,0,1:T(2,128)(2,1)}), bf16[2,32,2,7168]{3,2,0,1:T(2,128)(2,1)S(1)}, u32[]{:S(2)}, u32[]{:S(2)}) async-start(bf16[2,32,2,7168]{3,2,0,1:T(2,128)(2,1)} %copy.27), calls=%async_computation.3 | async-start | bytes 3670016 | tf_op jit(solution)/shard_map/all_to_all | solution.py:114
  248.4 0.0 copy-start.2
  248.4 0.0 copy-start.3
  248.5 0.0 copy-done.5
  248.5 0.1 iota_compare_fusion.1
  248.5 0.0 copy-done
  248.5 1.7 fusion.33
  250.2 0.0 copy-done.2
  250.2 0.0 copy-done.3
  250.2 0.3 fusion.5
  250.6 0.2 fusion.32
  250.8 1.7 convolution_convert_fusion.1
  252.5 21.5 %all-to-all-done.2 = bf16[2,32,2,7168]{3,2,0,1:T(2,128)(2,1)S(1)} async-done(((bf16[2,32,2,7168]{3,2,0,1:T(2,128)(2,1)}), bf16[2,32,2,7168]{3,2,0,1:T(2,128)(2,1)S(1)}, u32[]{:S(2)}, u32[]{:S(2)}) %all-to-all-start.2) | async-done | bytes 1835040 | tf_op jit(solution)/shard_map/all_to_all | solution.py:114
  273.9 2.5 copy.28
  276.4 4.1 %reshape.287 = bf16[128,7168]{1,0:T(8,128)(2,1)S(1)} reshape(bf16[2,32,2,7168]{3,2,1,0:T(2,128)(2,1)} %copy.28) | data formatting | bytes 3670016 | tf_op jit(solution)/shard_map/reshape | solution.py:121
  280.5 0.0 copy-start.4
  280.5 0.0 copy-start.1
  280.5 2.1 gather_fusion.1
  282.6 0.0 copy-done.4
  282.6 1.6 fusion.7
  284.2 0.0 copy-done.1
  284.2 0.7 fusion.19
  (8 shorter events, 0.1 us)
Async XLA Ops:
  7.2 241.4 %copy-start = (bf16[8,128,512]{2,1,0:T(8,128)(2,1)S(1)}, bf16[8,128,512]{2,1,0:T(8,128)(2,1)}, u32[]{:S(2)}) copy-start(bf16[8,128,512]{2,1,0:T(8,128)(2,1)} %param.14) | copy-start | bytes 3145732
  7.2 131.7 %all-gather.2.cloned.1.call-start = ((), (), s32[]{:S(2)}) async-start(), calls=%async_computation.4 | async-start | bytes 9175040 | tf_op jit(solution)/shard_map/all_gather | solution.py:108
  65.6 168.6 %reduce-scatter.2.cloned.1.call-start = ((), (), s32[]{:S(2)}) async-start(), calls=%async_computation.5 | async-start | bytes 9175040 | tf_op jit(solution)/shard_map/reduce_scatter | solution.py:111
  240.5 7.9 %copy-start.5 = (s32[8]{0:T(128)S(1)}, s32[8]{0:T(128)}, u32[]{:S(2)}) copy-start(s32[8]{0:T(128)} %param.16) | copy-start | bytes 100
  240.5 33.4 %all-to-all-start.2 = ((bf16[2,32,2,7168]{3,2,0,1:T(2,128)(2,1)}), bf16[2,32,2,7168]{3,2,0,1:T(2,128)(2,1)S(1)}, u32[]{:S(2)}, u32[]{:S(2)}) async-start(bf16[2,32,2,7168]{3,2,0,1:T(2,128)(2,1)} %copy.27), calls=%async_computation.3 | async-start | bytes 3670016 | tf_op jit(solution)/shard_map/all_to_all | solution.py:114
  248.4 1.8 copy-start.2
  248.4 1.8 copy-start.3
  280.5 2.1 copy-start.4
  280.5 3.6 %copy-start.1 = (bf16[8,7168]{1,0:T(8,128)(2,1)S(1)}, bf16[8,7168]{1,0:T(8,128)(2,1)}, u32[]{:S(2)}) copy-start(bf16[8,7168]{1,0:T(8,128)(2,1)} %param.17) | copy-start | bytes 344068
Sparse Core Ops, SparseCore 0:
  65.7 73.1 all-gather.1
  160.6 73.4 reduce-scatter.1
where the time goes:
time: 292 us
  waiting for transfers between devices  168 us (58%)
  blocking collectives  38.4 us (13%)
  local copies, waits for them, and re-layouts  29.2 us (10%)
  matrix products  26.8 us (9%)
  between operations  14.3 us (5%)
  starting transfers between devices  8.16 us (3%)
  other arithmetic  6.57 us (2%)
    reduce_scatter x1, waiting for transfers between devices, per_device(): lax.psum_scatter(partials.astype(jnp.float32).astype(jnp.bfloat16), 'rep'...  73.6 us
    all_gather x1, waiting for transfers between devices, per_device(): everyone = lax.all_gather(incoming, 'rep', axis=1, tiled=True)  73.1 us
    all_to_all x2, blocking collectives, moved_by_axis(): result = lax.all_to_all(result, axes[k], k, k, tiled=True)  38.4 us
    all_to_all x1, waiting for transfers between devices, per_device(): lax.all_to_all(summed.reshape(local_count, ep_count, capacity, feature_di...  21.5 us
    dot_general x1, matrix products, expert_block(): jnp.dot(hidden, down_part, preferred_element_type=jnp.float32)  14.3 us
    all_to_all x1, starting transfers between devices, per_device(): lax.all_to_all(summed.reshape(local_count, ep_count, capacity, feature_di...  7.9 us
    dot_general x1, matrix products, expert_block(): gate_act = jnp.dot(tokens_in, gate_part, preferred_element_type=jnp.float32)  7.22 us
    convert_element_type x2, local copies, waits for them, and re-layouts, per_device(): summed.reshape(local_count, ep_count, capacity, feature_dim)  6.39 us
  transfers between devices with their start and end apart: 3, of which 3 were waited for; matrix products, arithmetic and copies ran while one was open for 1% of the time, Pallas kernels for 0%

commit v1 on v0

--- a/solution.py
+++ b/solution.py
@@ -105,7 +105,15 @@
     attn_latent = jnp.einsum(
         "iht,itl->ihl", attn_weights, cache_latent, preferred_element_type=jnp.float32
     ).astype(jnp.bfloat16)
-    everyone = lax.all_gather(incoming, "rep", axis=1, tiled=True)
+    everyone = jnp.concatenate(
+        lax.all_to_all(
+            jnp.stack(lax.axis_size("rep") * [incoming], axis=0),
+            axis_name="rep",
+            split_axis=0,
+            concat_axis=0,
+        ),
+        axis=1,
+    )
     partials = jax.vmap(expert_block)(everyone, w_gate, w_up, w_down)
     partials = lax.optimization_barrier(partials)
     summed = lax.psum_scatter(

time: 292 us -> 307 us (1.051)
  blocking collectives: 38.4 us -> 123 us
  waiting for transfers between devices: 168 us -> 92.1 us
  local copies, waits for them, and re-layouts: 29.2 us -> 35.4 us
    all_to_all x0 -> x1, blocking collectives: none -> 84.3 us  [per_device(): lax.all_to_all(jnp.stack(lax.axis_size('rep') * [incoming], axis=0), axis...]
    all_gather x1 -> x0, waiting for transfers between devices: 73.1 us -> none  [per_device(): everyone = lax.all_gather(incoming, 'rep', axis=1, tiled=True)]
    reshape x0 -> x1, local copies, waits for them, and re-layouts: none -> 3.5 us  [per_device(): jnp.concatenate(lax.all_to_all(jnp.stack(lax.axis_size('rep') * [incoming...]
  transfers between devices with their start and end apart: 3 -> 2, of which waited for: 3 -> 2; matrix products, arithmetic and copies ran while one was open for 1% -> 2% of each run, Pallas kernels for 0% -> 0%
where the time goes in v1:
time: 307 us; the launch traced here: 306 us
  blocking collectives  123 us (40%)
  waiting for transfers between devices  92.1 us (30%)
  local copies, waits for them, and re-layouts  35.4 us (12%)
  matrix products  27.6 us (9%)
  between operations  14.3 us (5%)
  starting transfers between devices  7.8 us (3%)
  other arithmetic  6.57 us (2%)
    all_to_all x1, blocking collectives, per_device(): lax.all_to_all(jnp.stack(lax.axis_size('rep') * [incoming], axis=0), axis...  84.3 us
    reduce_scatter x1, waiting for transfers between devices, per_device(): lax.psum_scatter(partials.astype(jnp.float32).astype(jnp.bfloat16), 'rep'...  71.4 us
    all_to_all x2, blocking collectives, moved_by_axis(): result = lax.all_to_all(result, axes[k], k, k, tiled=True)  38.4 us
    all_to_all x1, waiting for transfers between devices, per_device(): lax.all_to_all(summed.reshape(local_count, ep_count, capacity, feature_di...  20.6 us
    dot_general x1, matrix products, expert_block(): jnp.dot(hidden, down_part, preferred_element_type=jnp.float32)  14.3 us
    all_to_all x1, starting transfers between devices, per_device(): lax.all_to_all(summed.reshape(local_count, ep_count, capacity, feature_di...  7.76 us
    dot_general x1, matrix products, expert_block(): gate_act = jnp.dot(tokens_in, gate_part, preferred_element_type=jnp.float32)  7.22 us
    convert_element_type x2, local copies, waits for them, and re-layouts, per_device(): summed.reshape(local_count, ep_count, capacity, feature_dim)  6.39 us
  transfers between devices with their start and end apart: 2, of which 2 were waited for; matrix products, arithmetic and copies ran while one was open for 2% of the time, Pallas kernels for 0%

profile of v1, /device:TPU:1, one launch (start us, length us, event | category | flops | bytes accessed | tf_op | source)
XLA Modules:
  0.0 306.5 jit_solution(13840302822940996875)
XLA Ops:
  7.2 0.0 copy-start
  7.2 0.0 reduce-scatter.2.cloned.1.call-start
  7.2 0.8 eq.29
  8.1 0.8 reshape.292
  8.8 0.1 fusion.20
  8.9 0.1 reduce_window_sum.11
  9.0 0.2 select_reduce_fusion
  9.2 0.8 scatter_custom_fusion
  10.0 1.1 fusion.16
  11.1 1.0 fusion.18
  12.1 1.7 gather_fusion
  13.8 1.7 gather.9
  15.5 1.0 scatter_custom_fusion.1
  16.5 0.1 mul.87
  16.7 3.1 %copy_multiply_fusion = bf16[2,32,1,2,7168]{4,3,0,1,2:T(2,128)(2,1)S(1)} fusion(bf16[2,32,1,2,7168]{4,3,1,0,2:T(2,128)(2,1)} %gather.9, bf16[2,32,2]{2,0,1:T(2,128)(2,1)S(1)} %copy.31), kind=kLoop, calls=%fused_computation.6 | loop fusion | flops 917504 | bytes 3670272 | tf_op jit(solution)/shard_map/mul | solution.py:47
  19.8 1.3 copy.33
  21.1 6.2 %all_to_all.20 = bf16[16,2,2,1,2,7168]{5,4,0,2,3,1:T(2,128)(2,1)S(1)} all-to-all(bf16[16,2,2,1,2,7168]{5,4,0,2,3,1:T(2,128)(2,1)S(1)} %copy.33), channel_id=1, replica_groups=mesh['rep'=4,'ep_0'=4,'ep_1'=4,'ep_2'=2] {'ep_2'}, dimensions={1} | all-to-all | bytes 3670016 | tf_op jit(solution)/shard_map/all_to_all | solution.py:28
  27.3 1.7 copy.34
  29.0 32.2 %all_to_all.21 = bf16[16,2,2,1,2,7168]{5,4,1,2,3,0:T(2,128)(2,1)S(1)} all-to-all(bf16[16,2,2,1,2,7168]{5,4,1,2,3,0:T(2,128)(2,1)S(1)} %copy.34), channel_id=1, replica_groups=mesh['rep'=4,'ep_0'=4,'ep_1'=4,'ep_2'=2] {'ep_0','ep_1'}, dimensions={0} | all-to-all | bytes 3670016 | tf_op jit(solution)/shard_map/all_to_all | solution.py:28
  61.2 1.3 copy.35
  62.5 1.4 copy.36
  64.0 0.4 copy.37
  64.3 3.9 %stack.3 = bf16[4,2,64,7168]{3,2,1,0:T(8,128)(2,1)} broadcast(bf16[2,64,7168]{2,1,0:T(8,128)(2,1)S(1)} %copy.37), dimensions={1,2,3} | broadcast | bytes 9175040 | tf_op jit(solution)/shard_map/stack | solution.py:110
  68.2 84.3 %all_to_all.22 = bf16[4,2,64,7168]{3,2,1,0:T(8,128)(2,1)S(1)} all-to-all(bf16[4,2,64,7168]{3,2,1,0:T(8,128)(2,1)} %stack.3), channel_id=1, replica_groups=mesh['rep'=4,'ep_0'=4,'ep_1'=4,'ep_2'=2] {'rep'}, dimensions={0} | all-to-all | bytes 14680064 | tf_op jit(solution)/shard_map/all_to_all | solution.py:109
  152.5 3.5 %copy.38 = bf16[2,4,64,7168]{3,2,1,0:T(8,128)(2,1)} copy(bf16[2,4,64,7168]{3,2,0,1:T(8,128)(2,1)S(1)} %bitcast.33) | data formatting | bytes 14680064 | tf_op jit(solution)/shard_map/reshape | solution.py:108
  156.0 7.2 %fusion.34 = f32[2,256,256]{2,1,0:T(8,128)S(1)} fusion(bf16[2,256,7168]{2,1,0:T(8,128)(2,1)} %bitcast.34, bf16[2,7168,256]{2,1,0:T(8,128)(2,1)} %param.21), kind=kOutput, calls=%fused_computation.65 | convolution fusion | flops 1879048192 | bytes 15204352 | tf_op jit(solution)/shard_map/vmap()/dot_general | solution.py:51
  163.2 14.3 %convolution_convert_fusion = bf16[2,256,7168]{2,1,0:T(8,128)(2,1)} fusion(bf16[2,256,7168]{2,1,0:T(8,128)(2,1)} %param.23, bf16[2,256,7168]{2,1,0:T(8,128)(2,1)} %bitcast.35, bf16[2,7168,256]{2,1,0:T(8,128)(2,1)} %param.22, f32[2,256,256]{2,1,0:T(8,128)S(1)} %fusion.34), kind=kOutput, calls=%fused_computation.5 | convolution fusion | flops 3762552832 | bytes 29884416 | tf_op jit(solution)/shard_map/vmap()/dot_general | solution.py:54
  177.5 0.0 reduce-scatter.2.cloned.1.call-update
  177.6 0.0 copy-start.4
  177.6 0.0 copy-start.2
  177.6 71.4 %reduce-scatter.2.cloned.1.call-done = bf16[2,64,7168]{2,1,0:T(8,128)(2,1)} async-done(((bf16[2,256,7168]{2,1,0:T(8,128)(2,1)}), bf16[2,64,7168]{2,1,0:T(8,128)(2,1)}) %reduce-scatter.2.cloned.1.call-update) | async-done | bytes 1835024 | tf_op jit(solution)/shard_map/reduce_scatter | solution.py:119
  249.0 3.9 %convert_element_type.52 = bf16[2,32,2,7168]{3,2,1,0:T(2,128)(2,1)S(1)} reshape(bf16[2,64,7168]{2,1,0:T(8,128)(2,1)} %reduce-scatter.2.cloned.1.call-done) | data formatting | bytes 3670016 | tf_op jit(solution)/shard_map/convert_element_type | solution.py:123
  252.9 2.5 copy.39
  255.4 7.8 %all-to-all-start.3 = ((bf16[2,32,2,7168]{3,2,0,1:T(2,128)(2,1)}), bf16[2,32,2,7168]{3,2,0,1:T(2,128)(2,1)S(1)}, u32[]{:S(2)}, u32[]{:S(2)}) async-start(bf16[2,32,2,7168]{3,2,0,1:T(2,128)(2,1)} %copy.39), calls=%async_computation.4 | async-start | bytes 3670016 | tf_op jit(solution)/shard_map/all_to_all | solution.py:122
  263.2 0.0 copy-done.4
  263.2 0.1 iota_compare_fusion.1
  263.3 0.0 copy-done
  263.3 1.6 fusion.33
  264.9 0.0 copy-done.2
  265.0 1.2 fusion.5
  266.2 0.2 fusion.32
  266.4 1.7 convolution_convert_fusion.1
  268.1 0.0 copy-start.3
  268.1 20.6 %all-to-all-done.3 = bf16[2,32,2,7168]{3,2,0,1:T(2,128)(2,1)S(1)} async-done(((bf16[2,32,2,7168]{3,2,0,1:T(2,128)(2,1)}), bf16[2,32,2,7168]{3,2,0,1:T(2,128)(2,1)S(1)}, u32[]{:S(2)}, u32[]{:S(2)}) %all-to-all-start.3) | async-done | bytes 1835040 | tf_op jit(solution)/shard_map/all_to_all | solution.py:122
  288.7 2.5 copy.40
  291.2 0.0 copy-start.1
  291.2 4.1 %reshape.297 = bf16[128,7168]{1,0:T(8,128)(2,1)S(1)} reshape(bf16[2,32,2,7168]{3,2,1,0:T(2,128)(2,1)} %copy.40) | data formatting | bytes 3670016 | tf_op jit(solution)/shard_map/reshape | solution.py:129
  295.3 2.1 gather_fusion.1
  297.4 0.0 copy-done.3
  297.4 1.6 fusion.7
  298.9 0.0 copy-done.1
  298.9 0.7 fusion.19
  (8 shorter events, 0.1 us)
Async XLA Ops:
  7.2 256.1 %copy-start = (bf16[8,128,512]{2,1,0:T(8,128)(2,1)S(1)}, bf16[8,128,512]{2,1,0:T(8,128)(2,1)}, u32[]{:S(2)}) copy-start(bf16[8,128,512]{2,1,0:T(8,128)(2,1)} %param.14) | copy-start | bytes 3145732
  7.2 241.8 %reduce-scatter.2.cloned.1.call-start = ((), (), s32[]{:S(2)}) async-start(), calls=%async_computation.5 | async-start | bytes 9175040 | tf_op jit(solution)/shard_map/reduce_scatter | solution.py:119
  177.6 85.7 %copy-start.4 = (s32[8]{0:T(128)S(1)}, s32[8]{0:T(128)}, u32[]{:S(2)}) copy-start(s32[8]{0:T(128)} %param.16) | copy-start | bytes 100
  177.6 87.4 %copy-start.2 = (bf16[8,128,64]{1,2,0:T(8,128)(2,1)S(1)}, bf16[8,128,64]{1,2,0:T(8,128)(2,1)}, u32[]{:S(2)}) copy-start(bf16[8,128,64]{1,2,0:T(8,128)(2,1)} %param.13) | copy-start | bytes 393220
  255.4 33.3 %all-to-all-start.3 = ((bf16[2,32,2,7168]{3,2,0,1:T(2,128)(2,1)}), bf16[2,32,2,7168]{3,2,0,1:T(2,128)(2,1)S(1)}, u32[]{:S(2)}, u32[]{:S(2)}) async-start(bf16[2,32,2,7168]{3,2,0,1:T(2,128)(2,1)} %copy.39), calls=%async_computation.4 | async-start | bytes 3670016 | tf_op jit(solution)/shard_map/all_to_all | solution.py:122
  268.1 29.3 %copy-start.3 = (bf16[8,8]{1,0:T(8,128)(2,1)S(1)}, bf16[8,8]{1,0:T(8,128)(2,1)}, u32[]{:S(2)}) copy-start(bf16[8,8]{1,0:T(8,128)(2,1)} %param.20) | copy-start | bytes 388
  291.2 7.7 %copy-start.1 = (bf16[8,7168]{1,0:T(8,128)(2,1)S(1)}, bf16[8,7168]{1,0:T(8,128)(2,1)}, u32[]{:S(2)}) copy-start(bf16[8,7168]{1,0:T(8,128)(2,1)} %param.17) | copy-start | bytes 344068
Sparse Core Ops, SparseCore 0:
  177.7 71.3 reduce-scatter.1
